TPU v7x, 256 devices: a whole 4x4x8 slice. The times are simulated.
256 devices in a mesh: row: 64 (over x, y_lo, z), panel: 4 (over y_hi, core).
Axes of the slice: x: 4, y: 4 (y_hi: 2, y_lo: 2; y = y_hi * 2 + y_lo), z: 8, core: 2. Of those that a mesh axis runs over, the one named last changes fastest.
Arguments:
- pixel_ids: int32 [65536], P('row'), may hold values from 0 to 65535, each once
- quad_offsets: int32 [2, 16, 65536], P(None, None, 'row'), may hold values from 0 to 7
- prior_factor: float32 [65536, 2048], P('row', 'panel'), may hold values from -0.036 to 0.036, as said below
Outputs:
- panel_factor: float32 [65536, 1024], P(('row', 'panel'))
Inputs may be any that keep to these rules, and one draw needn't show every extreme that they name: `pixel_ids`: each pixel of the grid appears in exactly one row. `prior_factor`: schur[panel_index] is positive definite.
All inputs are finite; a program needn't handle non-finite values.
Results may differ from a plain program's by a relative error of at most 0.0003.
Values sent between devices are 32-bit elements; how exact they have to be, the bound alone decides.
A program may use at most 128 MiB of HBM per device.

v0:
```python
import jax
import jax.numpy as jnp
from jax import lax
from jax.sharding import PartitionSpec as P

B = 1024
range_inverse = 1.0


def from_behind(block, axis, distance):
    devices = range(lax.axis_size(axis))
    route = [((i - distance) % len(devices), i) for i in devices]
    return lax.ppermute(block, axis, route)


def locate(pixel_ids, quad_offsets):
    column = (pixel_ids % 256).astype(jnp.float32)
    lines = (pixel_ids // 256).astype(jnp.float32)
    east = column[None, :] + (quad_offsets[0].astype(jnp.float32) + 0.5) / 8.0
    north = lines[None, :] + (quad_offsets[1].astype(jnp.float32) + 0.5) / 8.0
    return (east, north)


def cover_tile(east_rows, north_rows, east_cols, north_cols):
    count = east_rows.shape[0]

    def accumulate(index, running):
        east_one = lax.dynamic_index_in_dim(east_rows, index, 0, keepdims=False)
        north_one = lax.dynamic_index_in_dim(north_rows, index, 0, keepdims=False)
        apart_east = east_cols[:, :, None] - east_one[None, None, :]
        apart_north = north_cols[:, :, None] - north_one[None, None, :]
        return running + jnp.sum(
            jnp.exp(-(apart_east * apart_east + apart_north * apart_north) * range_inverse), axis=0
        )

    start = jnp.zeros((east_cols.shape[1], east_rows.shape[1]), jnp.float32)
    total = lax.fori_loop(0, count, accumulate, start)
    return total.T / float(count * count)


def local(pixel_ids, quad_offsets, prior_factor):
    panel_count = lax.axis_size("panel")
    row_count = lax.axis_size("row")
    block_rows = pixel_ids.shape[0]
    quarter_rows = block_rows // panel_count
    per_device = B // (row_count * panel_count)
    span_cols = panel_count * per_device
    row_pos = lax.axis_index("row")
    panel_pos = lax.axis_index("panel")
    east, north = locate(pixel_ids, quad_offsets)
    all_points = jnp.stack([east, north])
    own_points = lax.dynamic_slice_in_dim(all_points, panel_pos * quarter_rows, quarter_rows, 2)
    own_east = own_points[0]
    own_north = own_points[1]
    local_points = all_points.reshape(2, east.shape[0], panel_count, quarter_rows)[
        :, :, :, :per_device
    ]
    local_points = local_points.reshape(2, east.shape[0], span_cols)
    start_cols = jnp.zeros((quarter_rows, B), jnp.float32)

    def place(columns, held, source):
        tile = cover_tile(own_east, own_north, held[0], held[1])
        return lax.dynamic_update_slice(columns, tile, (jnp.int32(0), source * span_cols))

    def turn(index, carry):
        held, columns = carry
        columns = place(columns, held, (row_pos - index) % row_count)
        held = from_behind(held, "row", 1)
        return (held, columns)

    held, columns = lax.fori_loop(0, row_count - 1, turn, (local_points, start_cols))
    columns = place(columns, held, (row_pos - (row_count - 1)) % row_count)
    device_pos = row_pos * panel_count + panel_pos
    row_ids = jnp.arange(quarter_rows, dtype=jnp.int32)[:, None]
    col_ids = jnp.arange(B, dtype=jnp.int32)[None, :]
    on_diagonal = (row_ids < per_device) & (col_ids == device_pos * per_device + row_ids)
    cover = columns + jnp.where(on_diagonal, 1.0, 0.0).astype(jnp.float32)
    whole_rows = lax.all_to_all(prior_factor, "panel", split_axis=0, concat_axis=1, tiled=True)
    panel_prior = lax.all_gather(whole_rows[:per_device], ("row", "panel"), axis=0, tiled=True)
    update = jnp.dot(
        whole_rows,
        panel_prior.T,
        precision=lax.Precision.HIGHEST,
        preferred_element_type=jnp.float32,
    )
    schur = cover - update
    diag_rows = lax.all_gather(schur[:per_device], ("row", "panel"), axis=0, tiled=True)
    diag_factor = jnp.linalg.cholesky(diag_rows)
    return lax.linalg.triangular_solve(
        diag_factor, schur, left_side=False, lower=True, transpose_a=True
    )


def solution(mesh):
    return jax.shard_map(
        local,
        mesh=mesh,
        in_specs=(P("row"), P(None, None, "row"), P("row", "panel")),
        out_specs=P(("row", "panel"), None),
        check_vma=False,
    )
```

profile of v0, /device:TPU:32, one launch (start us, length us, event | category | flops | bytes accessed | tf_op | source)
XLA Modules:
  0.0 1338.7 jit_solution(4955843680710674743)
XLA Ops:
  11.4 26.9 %all-to-all-done = f32[4,256,512]{2,1,0:T(8,128)S(1)} async-done(((f32[4,256,512]{2,1,0:T(8,128)}), f32[4,256,512]{2,1,0:T(8,128)S(1)}, u32[]{:S(2)}, u32[]{:S(2)}) %all-to-all-start) | async-done | bytes 2097184 | tf_op jit(solution)/shard_map/all_to_all | solution.py:78
  39.1 497.6 %while.68 = (s32[]{:T(128)}, f32[2,16,16]{2,1,0:T(8,128)S(1)}, f32[256,1024]{0,1:T(8,128)S(1)}, f32[16,256]{1,0:T(8,128)S(1)}, f32[16,256]{1,0:T(8,128)S(1)}, /*...) while((s32[]{:T(128)}, f32[2,16,16]{2,1,0:T(8,128)S(1)}, ...), condition=%wide.region_4.5_spmd, body=%wide.region_0.4_spmd.sunk | while | flops 466965 | bytes 123403 | solution.py:71
  62.2 4.6 collective-permute-done
  70.2 4.7 collective-permute-done
  78.2 4.7 collective-permute-done
  86.2 4.8 collective-permute-done
  102.2 4.6 collective-permute-done
  110.1 4.6 collective-permute-done
  118.1 4.6 collective-permute-done
  126.0 4.6 collective-permute-done
  134.0 4.7 collective-permute-done
  150.0 4.6 collective-permute-done
  165.8 4.6 collective-permute-done
  181.8 4.6 collective-permute-done
  189.7 4.7 collective-permute-done
  197.7 4.7 collective-permute-done
  213.6 4.6 collective-permute-done
  221.6 4.7 collective-permute-done
  237.5 4.7 collective-permute-done
  253.5 4.7 collective-permute-done
  269.3 4.6 collective-permute-done
  277.3 4.7 collective-permute-done
  309.1 4.7 collective-permute-done
  333.0 4.7 collective-permute-done
  349.0 4.7 collective-permute-done
  364.9 4.6 collective-permute-done
  372.8 4.6 collective-permute-done
  380.8 4.6 collective-permute-done
  388.8 4.6 collective-permute-done
  396.7 4.7 collective-permute-done
  412.6 4.6 collective-permute-done
  420.6 4.6 collective-permute-done
  428.6 4.6 collective-permute-done
  436.5 4.6 collective-permute-done
  444.5 4.6 collective-permute-done
  452.4 4.6 collective-permute-done
  468.4 4.6 collective-permute-done
  476.3 4.6 collective-permute-done
  492.3 4.6 collective-permute-done
  500.2 4.6 collective-permute-done
  516.1 4.6 collective-permute-done
  545.9 10.2 reshape.138
  556.0 16.1 %convolution_subtract_fusion = f32[256,1024]{1,0:T(8,128)S(1)} fusion(f32[256,2048]{0,1:T(8,128)S(1)} %bitcast.152, f32[1024,2048]{1,0:T(8,128)} %reshape.138, f32[256,1024]{1,0:T(8,128)S(1)} %dynamic_update_slice.13, s32[256]{0:T(256)S(1)} %iota_add_fusion, pred[256]{0:T(512)(128)(4,1)S(1)} %iota_compare_fusion.4), kind=kOutput, calls=%fused_computation.15 | convolution fusion | flops 6443761664 | bytes 12584192 | tf_op jit(solution)/shard_map/dot_general | solution.py:80
  573.7 412.5 %all-gather.7.cloned.1.call-done = f32[256,4,1024]{2,1,0:T(4,128)} async-done(((f32[1,4,1024]{2,1,0:T(4,128)}), f32[256,4,1024]{2,1,0:T(4,128)}) %all-gather.7.cloned.1.call-update) | async-done | bytes 4194320 | tf_op jit(solution)/shard_map/all_gather | solution.py:87
  986.2 5.3 reshape.140
  991.5 5.8 copy.69
  1003.6 11.7 cholesky.223
  1017.9 9.8 custom-call.62
  1031.6 11.9 cholesky.244
  1044.2 9.8 custom-call.63
  1057.3 11.7 cholesky.468
  1069.7 9.8 custom-call.64
  1083.0 11.9 cholesky.487
  1095.5 9.8 custom-call.65
  1108.8 11.7 cholesky.506
  1121.2 10.2 custom-call.66
  1134.7 11.7 cholesky.526
  1147.0 9.8 custom-call.67
  1159.8 11.7 cholesky.546
  1172.2 9.8 custom-call.68
  1184.6 11.7 cholesky.564
  1207.3 4.9 select_select_fusion
  1212.2 22.8 %while.69 = (s32[]{:T(128)}, f32[1024,1024]{1,0:T(8,128)}, s32[8,2]{0,1:T(2,128)S(1)}, f32[8,128,128]{2,1,0:T(8,128)S(1)}, s32[]{:T(128)}) while((s32[]{:T(128)}, f32[1024,1024]{1,0:T(8,128)}, s32[8,2]{0,1:T(2,128)S(1)}, f32[8,128,128]{2,1,0:T(8,128)S(1)}, s32[]{:T(128)}) %tuple.176), condition=%wide.while_cond, body=%wide.while_body.sunk | while | flops 2 | bytes 131189 | solution.py:89
  1235.1 78.8 %custom-call.69 = f32[8,128,128]{1,2,0:T(8,128)S(1)} custom-call(f32[8,128,128]{2,1,0:T(8,128)S(1)} %get-tuple-element.405), custom_call_target="InvertDiagBlocksLowerTriangular" | custom-call | tf_op jit(solution)/shard_map/triangular_solve | solution.py:89
  (3597 shorter events, 577.0 us)
Async XLA Ops:
  6.5 31.8 %all-to-all-start = ((f32[4,256,512]{2,1,0:T(8,128)}), f32[4,256,512]{2,1,0:T(8,128)S(1)}, u32[]{:S(2)}, u32[]{:S(2)}) async-start(f32[4,256,512]{2,1,0:T(8,128)} %bitcast.153), calls=%async_computation | async-start | bytes 4194304 | tf_op jit(solution)/shard_map/all_to_all | solution.py:78
  11.1 534.7 %all-gather.5.cloned.1.call-start = ((), (), s32[]{:S(2)}) async-start(), calls=%async_computation.1 | async-start | bytes 8421376 | tf_op jit(solution)/shard_map/all_gather | solution.py:79
  39.0 947.2 %all-gather.7.cloned.1.call-start = ((), (), s32[]{:S(2)}) async-start(), calls=%async_computation.2 | async-start | bytes 4210688 | tf_op jit(solution)/shard_map/all_gather | solution.py:87
  50.9 8.0 collective-permute-start
  58.9 8.0 collective-permute-start
  66.8 8.0 collective-permute-start
  74.9 8.0 collective-permute-start
  82.9 8.1 collective-permute-start
  90.9 7.9 collective-permute-start
  98.8 8.0 collective-permute-start
  106.8 8.0 collective-permute-start
  114.8 8.0 collective-permute-start
  122.7 8.0 collective-permute-start
  130.7 8.0 collective-permute-start
  138.7 8.0 collective-permute-start
  146.7 8.0 collective-permute-start
  154.6 7.9 collective-permute-start
  162.5 8.0 collective-permute-start
  170.5 8.0 collective-permute-start
  178.5 8.0 collective-permute-start
  186.4 8.0 collective-permute-start
  194.4 8.0 collective-permute-start
  202.4 7.9 collective-permute-start
  210.3 8.0 collective-permute-start
  218.3 8.0 collective-permute-start
  226.3 7.9 collective-permute-start
  234.2 8.0 collective-permute-start
  242.2 7.9 collective-permute-start
  250.1 8.0 collective-permute-start
  258.1 7.9 collective-permute-start
  266.0 8.0 collective-permute-start
  274.0 8.0 collective-permute-start
  282.0 7.9 collective-permute-start
  290.0 7.9 collective-permute-start
  297.9 7.9 collective-permute-start
  305.8 8.0 collective-permute-start
  313.8 8.0 collective-permute-start
  321.8 7.9 collective-permute-start
  329.7 8.0 collective-permute-start
  337.7 7.9 collective-permute-start
  345.6 8.0 collective-permute-start
  353.6 8.0 collective-permute-start
  361.6 8.0 collective-permute-start
  369.5 8.0 collective-permute-start
  377.5 8.0 collective-permute-start
  385.4 8.0 collective-permute-start
  393.4 8.0 collective-permute-start
  401.4 7.9 collective-permute-start
  409.3 8.0 collective-permute-start
  417.3 8.0 collective-permute-start
  425.2 8.0 collective-permute-start
  433.2 8.0 collective-permute-start
  441.2 8.0 collective-permute-start
  449.1 8.0 collective-permute-start
  457.1 8.0 collective-permute-start
  465.1 8.0 collective-permute-start
  473.0 8.0 collective-permute-start
  481.0 8.0 collective-permute-start
  488.9 8.0 collective-permute-start
  496.9 8.0 collective-permute-start
  504.9 8.0 collective-permute-start
  512.8 8.0 collective-permute-start
  520.8 8.0 collective-permute-start
  528.7 8.0 collective-permute-start
  (9 other events, 141.6 us)
Sparse Core Ops, SparseCore 0:
  39.1 420.7 all-gather.4
  573.8 412.3 all-gather.6
where the time goes:
time: 1350 us; the launch traced here: 1340 us
  waiting for transfers between devices  722 us (53%)
  other arithmetic  416 us (31%)
  local copies, waits for them, and re-layouts  69 us (5%)
  matrix products  55.5 us (4%)
  loops' own time  45.9 us (3%)
  between operations  19.1 us (1%)
    all_gather x1, waiting for transfers between devices, local(): lax.all_gather(schur[:per_device], ('row', 'panel'), axis=0, tiled=True)  412 us
    ppermute x63, waiting for transfers between devices, from_behind(): return lax.ppermute(block, axis, route)  283 us
    another operation x31, other arithmetic, local(): diag_factor = jnp.linalg.cholesky(diag_rows)  173 us
    reduce_sum x1024, other arithmetic, accumulate(): jnp.sum(jnp.exp(-(apart_east * apart_east + apart_north * apart_north) *...  148 us
    another operation x3, other arithmetic, local(): lax.linalg.triangular_solve(diag_factor, schur, left_side=False, lower=Tr...  83.7 us
    another operation x64, loops' own time, cover_tile(): total = lax.fori_loop(0, count, accumulate, start)  43 us
  transfers between devices with their start and end apart: 66, of which 64 were waited for; matrix products, arithmetic and copies ran while one was open for 13% of the time, Pallas kernels for 0%

commit v1 on v0

--- a/solution.py
+++ b/solution.py
@@ -84,7 +84,15 @@
         preferred_element_type=jnp.float32,
     )
     schur = cover - update
-    diag_rows = lax.all_gather(schur[:per_device], ("row", "panel"), axis=0, tiled=True)
+    diag_rows = jnp.concatenate(
+        lax.all_to_all(
+            jnp.stack([schur[:per_device]] * lax.axis_size(("row", "panel"))),
+            ("row", "panel"),
+            0,
+            0,
+        ),
+        axis=0,
+    )
     diag_factor = jnp.linalg.cholesky(diag_rows)
     return lax.linalg.triangular_solve(
         diag_factor, schur, left_side=False, lower=True, transpose_a=True

time: 1350 us -> 1050 us (0.78)
  waiting for transfers between devices: 722 us -> 406 us
    all_gather x1 -> x0, waiting for transfers between devices: 412 us -> none  [local(): lax.all_gather(schur[:per_device], ('row', 'panel'), axis=0, tiled=True)]
    all_to_all x0 -> x1, waiting for transfers between devices: none -> 96.2 us  [local(): lax.all_to_all(jnp.stack([schur[:per_device]] * lax.axis_size(('row', 'pa...]
  transfers between devices with their start and end apart: 66 -> 66, of which waited for: 64 -> 64; matrix products, arithmetic and copies ran while one was open for 13% -> 17% of each run, Pallas kernels for 0% -> 0%
where the time goes in v1:
time: 1050 us; the launch traced here: 1040 us
  other arithmetic  416 us (40%)
  waiting for transfers between devices  406 us (39%)
  local copies, waits for them, and re-layouts  71.2 us (7%)
  matrix products  55.5 us (5%)
  loops' own time  45.9 us (4%)
  starting transfers between devices  23.9 us (2%)
  between operations  19.3 us (2%)
    ppermute x63, waiting for transfers between devices, from_behind(): return lax.ppermute(block, axis, route)  283 us
    another operation x31, other arithmetic, local(): diag_factor = jnp.linalg.cholesky(diag_rows)  173 us
    reduce_sum x1024, other arithmetic, accumulate(): jnp.sum(jnp.exp(-(apart_east * apart_east + apart_north * apart_north) *...  148 us
    all_to_all x1, waiting for transfers between devices, local(): lax.all_to_all(jnp.stack([schur[:per_device]] * lax.axis_size(('row', 'pa...  96.2 us
    another operation x3, other arithmetic, local(): lax.linalg.triangular_solve(diag_factor, schur, left_side=False, lower=Tr...  83.7 us
    another operation x64, loops' own time, cover_tile(): total = lax.fori_loop(0, count, accumulate, start)  43 us
    all_to_all x1, waiting for transfers between devices, local(): lax.all_to_all(prior_factor, 'panel', split_axis=0, concat_axis=1, tiled=...  26.9 us
    another operation x14, matrix products, local(): diag_factor = jnp.linalg.cholesky(diag_rows)  23.1 us
  transfers between devices with their start and end apart: 66, of which 64 were waited for; matrix products, arithmetic and copies ran while one was open for 17% of the time, Pallas kernels for 0%

profile of v1, /device:TPU:32, one launch (start us, length us, event | category | flops | bytes accessed | tf_op | source)
XLA Modules:
  0.0 1038.0 jit_solution(3331568839337147262)
XLA Ops:
  11.4 26.9 %all-to-all-done = f32[4,256,512]{2,1,0:T(8,128)S(1)} async-done(((f32[4,256,512]{2,1,0:T(8,128)}), f32[4,256,512]{2,1,0:T(8,128)S(1)}, u32[]{:S(2)}, u32[]{:S(2)}) %all-to-all-start) | async-done | bytes 2097184 | tf_op jit(solution)/shard_map/all_to_all | solution.py:78
  39.0 497.6 %while.68 = (s32[]{:T(128)}, f32[2,16,16]{2,1,0:T(8,128)S(1)}, f32[256,1024]{0,1:T(8,128)S(1)}, f32[16,256]{1,0:T(8,128)S(1)}, f32[16,256]{1,0:T(8,128)S(1)}, /*...) while((s32[]{:T(128)}, f32[2,16,16]{2,1,0:T(8,128)S(1)}, ...), condition=%wide.region_4.5_spmd, body=%wide.region_0.4_spmd.sunk | while | flops 466965 | bytes 123403 | solution.py:71
  62.1 4.6 collective-permute-done
  70.1 4.7 collective-permute-done
  86.0 4.8 collective-permute-done
  102.1 4.6 collective-permute-done
  110.1 4.7 collective-permute-done
  126.0 4.6 collective-permute-done
  134.0 4.7 collective-permute-done
  149.9 4.6 collective-permute-done
  157.8 4.7 collective-permute-done
  173.8 4.6 collective-permute-done
  181.7 4.6 collective-permute-done
  189.7 4.7 collective-permute-done
  213.6 4.7 collective-permute-done
  221.5 4.7 collective-permute-done
  245.4 4.7 collective-permute-done
  253.4 4.6 collective-permute-done
  269.3 4.6 collective-permute-done
  277.3 4.7 collective-permute-done
  301.1 4.7 collective-permute-done
  325.0 4.7 collective-permute-done
  333.0 4.7 collective-permute-done
  356.9 4.6 collective-permute-done
  364.8 4.7 collective-permute-done
  380.7 4.6 collective-permute-done
  388.7 4.6 collective-permute-done
  396.7 4.7 collective-permute-done
  412.6 4.6 collective-permute-done
  420.6 4.7 collective-permute-done
  436.5 4.6 collective-permute-done
  444.4 4.6 collective-permute-done
  452.4 4.6 collective-permute-done
  460.4 4.6 collective-permute-done
  468.3 4.6 collective-permute-done
  476.3 4.6 collective-permute-done
  484.2 4.6 collective-permute-done
  500.2 4.6 collective-permute-done
  516.1 4.6 collective-permute-done
  524.0 4.6 collective-permute-done
  545.8 10.2 reshape.144
  556.0 16.1 %convolution_subtract_fusion = f32[256,1024]{1,0:T(8,128)S(1)} fusion(f32[256,2048]{0,1:T(8,128)S(1)} %bitcast.150, f32[1024,2048]{1,0:T(8,128)} %reshape.144, f32[256,1024]{1,0:T(8,128)S(1)} %dynamic_update_slice.13, s32[256]{0:T(256)S(1)} %iota_add_fusion, pred[256]{0:T(512)(128)(4,1)S(1)} %iota_compare_fusion.4), kind=kOutput, calls=%fused_computation.15 | convolution fusion | flops 6443761664 | bytes 12584192 | tf_op jit(solution)/shard_map/dot_general | solution.py:80
  576.1 13.2 %all-to-all-start.1 = ((f32[256,4,1024]{2,1,0:T(4,128)}), f32[256,4,1024]{2,1,0:T(4,128)}, u32[]{:S(2)}, u32[]{:S(2)}) async-start(f32[256,4,1024]{2,1,0:T(4,128)} %stack.14), calls=%async_computation.1 | async-start | bytes 8388608 | tf_op jit(solution)/shard_map/all_to_all | solution.py:88
  589.3 96.2 %all-to-all-done.1 = f32[256,4,1024]{2,1,0:T(4,128)} async-done(((f32[256,4,1024]{2,1,0:T(4,128)}), f32[256,4,1024]{2,1,0:T(4,128)}, u32[]{:S(2)}, u32[]{:S(2)}) %all-to-all-start.1) | async-done | bytes 4194336 | tf_op jit(solution)/shard_map/all_to_all | solution.py:88
  685.5 5.3 reshape.119
  690.7 5.5 copy.69
  702.6 11.7 %cholesky.223 = f32[128,128]{1,0:T(8,128)S(1)} custom-call(f32[128,128]{1,0:T(8,128)S(1)} %cholesky.580), custom_call_target="Cholesky" | custom-call | tf_op jit(solution)/shard_map/jit(cholesky)/cholesky | solution.py:96
  716.9 9.8 custom-call.62
  730.6 11.9 %cholesky.244 = f32[128,128]{1,0:T(8,128)S(1)} custom-call(f32[128,128]{1,0:T(8,128)S(1)} %cholesky.584), custom_call_target="Cholesky" | custom-call | tf_op jit(solution)/shard_map/jit(cholesky)/cholesky | solution.py:96
  743.2 9.8 custom-call.63
  756.3 11.7 %cholesky.468 = f32[128,128]{1,0:T(8,128)S(1)} custom-call(f32[128,128]{1,0:T(8,128)S(1)} %cholesky.589), custom_call_target="Cholesky" | custom-call | tf_op jit(solution)/shard_map/jit(cholesky)/cholesky | solution.py:96
  768.7 9.8 custom-call.64
  782.0 12.1 %cholesky.487 = f32[128,128]{1,0:T(8,128)S(1)} custom-call(f32[128,128]{1,0:T(8,128)S(1)} %cholesky.594), custom_call_target="Cholesky" | custom-call | tf_op jit(solution)/shard_map/jit(cholesky)/cholesky | solution.py:96
  794.7 9.8 custom-call.65
  808.0 11.7 %cholesky.506 = f32[128,128]{1,0:T(8,128)S(1)} custom-call(f32[128,128]{1,0:T(8,128)S(1)} %cholesky.599), custom_call_target="Cholesky" | custom-call | tf_op jit(solution)/shard_map/jit(cholesky)/cholesky | solution.py:96
  820.4 10.0 custom-call.66
  833.7 11.7 %cholesky.526 = f32[128,128]{1,0:T(8,128)S(1)} custom-call(f32[128,128]{1,0:T(8,128)S(1)} %cholesky.604), custom_call_target="Cholesky" | custom-call | tf_op jit(solution)/shard_map/jit(cholesky)/cholesky | solution.py:96
  846.0 9.8 custom-call.67
  858.8 11.7 %cholesky.546 = f32[128,128]{1,0:T(8,128)S(1)} custom-call(f32[128,128]{1,0:T(8,128)S(1)} %cholesky.609), custom_call_target="Cholesky" | custom-call | tf_op jit(solution)/shard_map/jit(cholesky)/cholesky | solution.py:96
  871.2 9.8 custom-call.68
  883.6 11.7 %cholesky.564 = f32[128,128]{1,0:T(8,128)S(1)} custom-call(f32[128,128]{1,0:T(8,128)S(1)} %convolution_subtract_fusion.14), custom_call_target="Cholesky" | custom-call | tf_op jit(solution)/shard_map/jit(cholesky)/cholesky | solution.py:96
  906.3 4.9 select_select_fusion
  911.2 22.8 %while.69 = (s32[]{:T(128)}, f32[1024,1024]{1,0:T(8,128)}, s32[8,2]{0,1:T(2,128)S(1)}, f32[8,128,128]{2,1,0:T(8,128)S(1)}, s32[]{:T(128)}) while((s32[]{:T(128)}, f32[1024,1024]{1,0:T(8,128)}, s32[8,2]{0,1:T(2,128)S(1)}, f32[8,128,128]{2,1,0:T(8,128)S(1)}, s32[]{:T(128)}) %tuple.176), condition=%wide.while_cond, body=%wide.while_body.sunk | while | flops 2 | bytes 131189 | solution.py:97
  934.0 78.8 %custom-call.69 = f32[8,128,128]{1,2,0:T(8,128)S(1)} custom-call(f32[8,128,128]{2,1,0:T(8,128)S(1)} %get-tuple-element.405), custom_call_target="InvertDiagBlocksLowerTriangular" | custom-call | tf_op jit(solution)/shard_map/triangular_solve | solution.py:97
  (3597 shorter events, 583.8 us)
Async XLA Ops:
  6.5 31.8 %all-to-all-start = ((f32[4,256,512]{2,1,0:T(8,128)}), f32[4,256,512]{2,1,0:T(8,128)S(1)}, u32[]{:S(2)}, u32[]{:S(2)}) async-start(f32[4,256,512]{2,1,0:T(8,128)} %bitcast.151), calls=%async_computation | async-start | bytes 4194304 | tf_op jit(solution)/shard_map/all_to_all | solution.py:78
  11.1 534.7 %all-gather.3.cloned.1.call-start = ((), (), s32[]{:S(2)}) async-start(), calls=%async_computation.2 | async-start | bytes 8421376 | tf_op jit(solution)/shard_map/all_gather | solution.py:79
  50.9 8.0 collective-permute-start
  58.8 8.0 collective-permute-start
  66.8 8.0 collective-permute-start
  74.8 7.9 collective-permute-start
  82.7 8.2 collective-permute-start
  90.9 7.9 collective-permute-start
  98.8 8.0 collective-permute-start
  106.8 8.0 collective-permute-start
  114.8 7.9 collective-permute-start
  122.7 8.0 collective-permute-start
  130.6 8.0 collective-permute-start
  138.6 7.9 collective-permute-start
  146.6 8.0 collective-permute-start
  154.5 8.0 collective-permute-start
  162.5 7.9 collective-permute-start
  170.4 8.0 collective-permute-start
  178.4 8.0 collective-permute-start
  186.4 8.0 collective-permute-start
  194.4 7.9 collective-permute-start
  202.3 7.9 collective-permute-start
  210.3 8.0 collective-permute-start
  218.2 8.0 collective-permute-start
  226.3 7.9 collective-permute-start
  234.2 7.9 collective-permute-start
  242.1 8.0 collective-permute-start
  250.1 8.0 collective-permute-start
  258.1 7.9 collective-permute-start
  266.0 8.0 collective-permute-start
  273.9 8.0 collective-permute-start
  282.0 7.9 collective-permute-start
  289.9 7.9 collective-permute-start
  297.8 8.0 collective-permute-start
  305.8 7.9 collective-permute-start
  313.8 7.9 collective-permute-start
  321.7 8.0 collective-permute-start
  329.7 8.0 collective-permute-start
  337.7 7.9 collective-permute-start
  345.6 7.9 collective-permute-start
  353.6 8.0 collective-permute-start
  361.5 8.0 collective-permute-start
  369.5 7.9 collective-permute-start
  377.4 8.0 collective-permute-start
  385.4 8.0 collective-permute-start
  393.4 8.0 collective-permute-start
  401.4 7.9 collective-permute-start
  409.3 8.0 collective-permute-start
  417.2 8.0 collective-permute-start
  425.2 7.9 collective-permute-start
  433.2 8.0 collective-permute-start
  441.1 8.0 collective-permute-start
  449.1 8.0 collective-permute-start
  457.0 8.0 collective-permute-start
  465.0 8.0 collective-permute-start
  473.0 8.0 collective-permute-start
  480.9 8.0 collective-permute-start
  488.9 8.0 collective-permute-start
  496.9 8.0 collective-permute-start
  504.8 8.0 collective-permute-start
  512.8 8.0 collective-permute-start
  520.7 8.0 collective-permute-start
  528.7 8.0 collective-permute-start
  576.1 109.4 %all-to-all-start.1 = ((f32[256,4,1024]{2,1,0:T(4,128)}), f32[256,4,1024]{2,1,0:T(4,128)}, u32[]{:S(2)}, u32[]{:S(2)}) async-start(f32[256,4,1024]{2,1,0:T(4,128)} %stack.14), calls=%async_computation.1 | async-start | bytes 8388608 | tf_op jit(solution)/shard_map/all_to_all | solution.py:88
  (9 other events, 141.6 us)
Sparse Core Ops, SparseCore 0:
  39.1 420.9 all-gather.2
